TPU v7x, 512 devices: a whole 4x8x8 slice. The times are simulated.
512 devices in a mesh: lon: 64 (over z_hi, x, y), ch: 8 (over z_lo, core).
Axes of the slice: x: 4, y: 8, z: 8 (z_hi: 2, z_lo: 4; z = z_hi * 4 + z_lo), core: 2. Of those that a mesh axis runs over, the one named last changes fastest.
Arguments:
- coarse: bfloat16 [16, 4, 256, 1024], P(None, None, 'lon', 'ch'), may hold values from -6 to 6
- up_kernel: bfloat16 [4, 4, 1024, 512], P(None, None, 'ch', 'lon'), may hold values from -0.09375 to 0.09375
- up_bias: float32 [512], replicated, may hold values from -3 to 3
- conv_kernel: bfloat16 [3, 3, 512, 512], P(None, None, 'lon'), may hold values from -0.09375 to 0.09375
- conv_bias: float32 [512], replicated, may hold values from -3 to 3
Outputs:
- fine_out: bfloat16 [32, 4, 512, 512], P('ch', None, 'lon')
All inputs are finite; a program needn't handle non-finite values.
Results may differ from a plain program's by a relative error of at most 0.015.
Values may be sent and summed in bfloat16 or wider, within the bound.
A program may use at most 64 MiB of HBM per device.

v0:
```python
import jax
import jax.numpy as jnp
from jax import lax
from jax.sharding import PartitionSpec as P

TAPS = (((1, 1), (3, 0)), ((2, 1), (0, 2)))


def padded_2(block, sides, width, periodic):
    for axis, dim in sides:
        count = lax.axis_size(axis)
        forward = [(i, i + 1) for i in range(count - 1)]
        if periodic:
            forward.append((count - 1, 0))
        backward = [(target, source) for source, target in forward]
        low = lax.ppermute(
            lax.slice_in_dim(block, block.shape[dim] - width, None, axis=dim), axis, forward
        )
        high = lax.ppermute(lax.slice_in_dim(block, 0, width, axis=dim), axis, backward)
        block = jnp.concatenate([low, block, high], axis=dim)
    return block


def tap_dot(piece, weight):
    return jnp.einsum("rbjc,cn->rbjn", piece, weight, preferred_element_type=jnp.float32)


def upsample(padded, lon_count, weights):
    rows = padded.shape[0] - 2
    batch = padded.shape[1]
    phases = []
    for p in range(2):
        columns = []
        for q in range(2):
            total = None
            for a, row_off in TAPS[p]:
                for c, col_off in TAPS[q]:
                    piece = padded[row_off : row_off + rows, :, col_off : col_off + lon_count, :]
                    term = tap_dot(piece, weights[a, c])
                    total = term if total is None else total + term
            columns.append(total)
        phases.append(jnp.stack(columns, axis=3))
    stacked = jnp.stack(phases, axis=1)
    return stacked.reshape(2 * rows, batch, 2 * lon_count, weights.shape[-1])


def shards(coarse, up_kernel, up_bias, conv_kernel, conv_bias):
    lon_dev = coarse.shape[2]
    row_padded = jnp.pad(coarse, ((1, 1), (0, 0), (0, 0), (0, 0)))
    source = jnp.pad(row_padded, ((0, 0), (0, 0), (2, 2), (0, 0)))
    count = lon_dev + 2
    up_full = lax.all_gather(up_kernel, "lon", axis=3, tiled=True)
    partial_value = upsample(source, count, up_full)
    local_fine = partial_value[:, :, 2 : 2 * lon_dev + 2]
    spill = jnp.concatenate(
        [partial_value[:, :, 1:2], partial_value[:, :, 2 * lon_dev + 2 : 2 * lon_dev + 3]], axis=2
    )
    beside_all = padded_2(spill.astype(jnp.bfloat16), (("lon", 2),), 1, True).astype(spill.dtype)
    local_fine = local_fine.at[:, :, 0].add(beside_all[:, :, 0])
    local_fine = local_fine.at[:, :, -1].add(beside_all[:, :, 3])
    summed = lax.psum_scatter(
        local_fine.astype(jnp.bfloat16), "ch", scatter_dimension=0, tiled=True
    ).astype(jnp.float32)
    hidden = jax.nn.gelu(summed + up_bias, approximate=False).astype(jnp.bfloat16)
    widened = padded_2(hidden, (("lon", 2),), 1, True)
    framed = padded_2(widened, (("ch", 0),), 1, False)
    weights = lax.all_gather(conv_kernel, "lon", axis=2, tiled=True)
    band_rows = hidden.shape[0]
    fine_cols = hidden.shape[2]
    result = jnp.zeros(hidden.shape, jnp.float32) + conv_bias
    for d in range(3):
        for t in range(3):
            result = result + tap_dot(
                framed[d : d + band_rows, :, t : t + fine_cols, :], weights[d, t]
            )
    return result.astype(jnp.bfloat16)


def solution(mesh):
    return jax.shard_map(
        shards,
        mesh=mesh,
        in_specs=(
            P(None, None, "lon", "ch"),
            P(None, None, "ch", "lon"),
            P(),
            P(None, None, "lon", None),
            P(),
        ),
        out_specs=P("ch", None, "lon", None),
        check_vma=False,
    )
```

profile of v0, /device:TPU:2, one launch (start us, length us, event | category | flops | bytes accessed | tf_op | source)
XLA Modules:
  0.0 451.6 jit_solution(3137635655831633041)
XLA Ops:
  6.5 1.4 copy.15
  8.0 0.9 copy.14
  8.9 146.6 %all-gather.3.cloned.1.call-done = bf16[4,4,128,512]{2,1,0,3:T(4,128)(2,1)} async-done(((bf16[4,4,128,8]{2,1,0,3:T(4,128)(2,1)}), bf16[4,4,128,512]{2,1,0,3:T(4,128)(2,1)}) %all-gather.3.cloned.1.call-update) | async-done | bytes 2097168 | tf_op jit(solution)/shard_map/all_gather | solution.py:52
  155.5 8.8 %fusion.77 = (bf16[1,1,128,512]{2,1,0,3:T(2,128)(2,1)S(1)}, bf16[1,1,128,512]{2,1,0,3:T(2,128)(2,1)S(1)}, bf16[1,1,128,512]{2,1,0,3:T(2,128)(2,1)}, bf16[1,1,128...) fusion(bf16[4,4,128,512]{2,1,0,3:T(4,128)(2,1)} %all-gather.3.c, ...), kind=kLoop, calls=%fused_computation.133 | loop fusion | bytes 4194304 | tf_op jit(solution)/shard_map/slice | solution.py:39
  164.3 0.8 copy.69
  165.1 0.8 copy.70
  165.9 0.8 copy.71
  166.6 0.8 copy.72
  167.4 0.8 copy.73
  168.2 1.1 fusion.50
  169.4 1.1 fusion.45
  170.5 1.7 copy.74
  172.2 0.8 copy.75
  173.0 0.8 copy.76
  173.8 0.8 copy.61
  174.6 1.1 fusion.60
  175.7 1.7 copy.62
  177.5 0.8 copy.63
  178.3 0.8 copy.64
  179.0 0.8 copy.65
  179.8 1.1 fusion.55
  181.0 1.7 copy.66
  182.7 1.7 copy.67
  184.4 0.8 copy.68
  185.2 1.2 convolution_add_fusion.5
  186.4 1.2 convolution_add_fusion.4
  187.7 0.3 fusion.1
  190.1 0.2 fusion.2
  190.3 0.4 maximum_bitcast_fusion
  190.7 0.3 pad_maximum_fusion
  191.0 2.0 copy.32
  193.0 0.9 copy.78
  193.9 0.5 fusion.76
  194.5 2.4 collective-permute-start
  196.8 5.8 %collective-permute-start.1 = (bf16[32,4,1,512]{3,2,1,0:T(2,128)(2,1)S(1)}, bf16[32,4,1,512]{3,2,1,0:T(2,128)(2,1)S(1)}, u32[]{:S(2)}, u32[]{:S(2)}) collective-permute-start(bf16[32,4,1,512]{3,2,1,0:T(2,128)(2,1)S(1)} %get-tuple-element.30), channel_id=1, source_target_pairs={{8,0},{16,8},{24,16},{32,24},{40,32},{48,40},{56,48},{64,56},{72,6... | collective-permute-start | bytes 393224 | tf_op jit(solution)/shard_map/ppermute | solution.py:19
  202.6 1.3 copy.33
  203.9 0.5 slice.296
  204.4 0.4 collective-permute-done
  204.8 1.5 collective-permute-done.1
  206.3 1.4 convert_add_fusion
  207.7 2.1 scatter-add.6
  209.8 1.4 fusion.23
  211.2 2.1 scatter-add.9
  213.3 1.2 convert_element_type.21
  214.5 0.7 all-gather.5.cloned.1.call-update
  215.2 47.2 %reduce-scatter.2.cloned.1.call-done = bf16[4,4,8,512]{3,2,1,0:T(8,128)(2,1)} async-done(((bf16[32,4,8,512]{3,2,1,0:T(8,128)(2,1)}), bf16[4,4,8,512]{3,2,1,0:T(8,128)(2,1)}) %reduce-scatter.2.cloned.1.call-update) | async-done | bytes 131088 | tf_op jit(solution)/shard_map/reduce_scatter | solution.py:61
  262.4 1.5 fusion.21
  263.9 3.4 collective-permute-start.2
  267.3 4.6 %collective-permute-start.3 = (bf16[4,4,1,512]{3,2,1,0:T(2,128)(2,1)S(1)}, bf16[4,4,1,512]{3,2,1,0:T(2,128)(2,1)S(1)}, u32[]{:S(2)}, u32[]{:S(2)}) collective-permute-start(bf16[4,4,1,512]{3,2,1,0:T(2,128)(2,1)S(1)} %get-tuple-element.52), channel_id=1, source_target_pairs={{8,0},{16,8},{24,16},{32,24},{40,32},{48,40},{56,48},{64,56},{72,6... | collective-permute-start | bytes 49160 | tf_op jit(solution)/shard_map/ppermute | solution.py:19
  271.9 1.6 collective-permute-done.3
  273.6 1.3 collective-permute-start.4
  274.9 1.3 collective-permute-start.5
  276.2 1.8 collective-permute-done.5
  278.0 0.2 maximum_maximum_fusion
  278.3 154.6 %all-gather.5.cloned.1.call-done = bf16[3,3,512,512]{3,2,1,0:T(8,128)(2,1)} async-done(((bf16[3,3,8,512]{3,2,1,0:T(8,128)(2,1)}), bf16[3,3,512,512]{3,2,1,0:T(8,128)(2,1)}) %all-gather.5.cloned.1.call-update) | async-done | bytes 4718608 | tf_op jit(solution)/shard_map/all_gather | solution.py:67
  432.8 1.3 fusion.16
  434.1 1.3 fusion.17
  435.4 1.3 fusion.18
  436.7 1.3 fusion.15
  438.0 1.3 fusion.13
  439.2 1.3 fusion.14
  440.5 1.3 fusion.12
  441.8 1.3 fusion.10
  443.1 2.0 fusion.11
  (41 shorter events, 2.2 us)
Async XLA Ops:
  6.5 149.0 %all-gather.3.cloned.1.call-start = ((), (), s32[]{:S(2)}) async-start(), calls=%async_computation.1 | async-start | bytes 2129920 | tf_op jit(solution)/shard_map/all_gather | solution.py:52
  7.9 254.4 %reduce-scatter.2.cloned.1.call-start = ((), (), s32[]{:S(2)}) async-start(), calls=%async_computation.2 | async-start | bytes 1179648 | tf_op jit(solution)/shard_map/reduce_scatter | solution.py:61
  185.2 2.4 copy-start
  185.2 2.7 copy-start.2
  185.2 3.0 copy-start.3
  186.4 2.0 copy-start.1
  187.6 1.1 copy-start.5
  187.9 1.1 copy-start.6
  188.2 1.1 copy-start.4
  188.5 1.1 copy-start.8
  188.7 1.1 copy-start.9
  189.0 1.0 copy-start.7
  194.5 10.4 %collective-permute-start = (bf16[32,4,1,512]{3,2,1,0:T(2,128)(2,1)S(1)}, bf16[32,4,1,512]{3,2,1,0:T(2,128)(2,1)S(1)}, u32[]{:S(2)}, u32[]{:S(2)}) collective-permute-start(bf16[32,4,1,512]{3,2,1,0:T(2,128)(2,1)S(1)} %get-tuple-element.29), channel_id=1, source_target_pairs={{0,8},{8,16},{16,24},{24,32},{32,40},{40,48},{48,56},{56,64},{64,7... | collective-permute-start | bytes 393224 | tf_op jit(solution)/shard_map/ppermute | solution.py:16
  196.8 9.5 %collective-permute-start.1 = (bf16[32,4,1,512]{3,2,1,0:T(2,128)(2,1)S(1)}, bf16[32,4,1,512]{3,2,1,0:T(2,128)(2,1)S(1)}, u32[]{:S(2)}, u32[]{:S(2)}) collective-permute-start(bf16[32,4,1,512]{3,2,1,0:T(2,128)(2,1)S(1)} %get-tuple-element.30), channel_id=1, source_target_pairs={{8,0},{16,8},{24,16},{32,24},{40,32},{48,40},{56,48},{64,56},{72,6... | collective-permute-start | bytes 393224 | tf_op jit(solution)/shard_map/ppermute | solution.py:19
  209.8 52.6 %copy-start.10 = (f32[512]{0:T(512)S(1)}, f32[512]{0:T(512)}, u32[]{:S(2)}) copy-start(f32[512]{0:T(512)} %param.11) | copy-start | bytes 6148
  214.5 218.3 %all-gather.5.cloned.1.call-start = ((), (), s32[]{:S(2)}) async-start(), calls=%async_computation.3 | async-start | bytes 4792320 | tf_op jit(solution)/shard_map/all_gather | solution.py:67
  263.9 8.0 %collective-permute-start.2 = (bf16[4,4,1,512]{3,2,1,0:T(2,128)(2,1)S(1)}, bf16[4,4,1,512]{3,2,1,0:T(2,128)(2,1)S(1)}, u32[]{:S(2)}, u32[]{:S(2)}) collective-permute-start(bf16[4,4,1,512]{3,2,1,0:T(2,128)(2,1)S(1)} %get-tuple-element.51), channel_id=1, source_target_pairs={{0,8},{8,16},{16,24},{24,32},{32,40},{40,48},{48,56},{56,64},{64,7... | collective-permute-start | bytes 49160 | tf_op jit(solution)/shard_map/ppermute | solution.py:16
  267.3 6.1 %collective-permute-start.3 = (bf16[4,4,1,512]{3,2,1,0:T(2,128)(2,1)S(1)}, bf16[4,4,1,512]{3,2,1,0:T(2,128)(2,1)S(1)}, u32[]{:S(2)}, u32[]{:S(2)}) collective-permute-start(bf16[4,4,1,512]{3,2,1,0:T(2,128)(2,1)S(1)} %get-tuple-element.52), channel_id=1, source_target_pairs={{8,0},{16,8},{24,16},{32,24},{40,32},{48,40},{56,48},{64,56},{72,6... | collective-permute-start | bytes 49160 | tf_op jit(solution)/shard_map/ppermute | solution.py:19
  273.6 2.6 collective-permute-start.4
  274.9 3.1 collective-permute-start.5
  278.3 163.5 %copy-start.11 = (f32[512]{0:T(512)S(1)}, f32[512]{0:T(512)}, u32[]{:S(2)}) copy-start(f32[512]{0:T(512)} %param.13) | copy-start | bytes 6148
Sparse Core Ops, SparseCore 0:
  11.8 143.6 all-gather.2
  214.6 47.7 reduce-scatter.1
  266.7 166.0 all-gather.4
where the time goes:
time: 453 us; the launch traced here: 452 us
  waiting for transfers between devices  354 us (78%)
  local copies, waits for them, and re-layouts  36.9 us (8%)
  matrix products  21.6 us (5%)
  starting transfers between devices  18.8 us (4%)
  between operations  13.6 us (3%)
  other arithmetic  6.35 us (1%)
    all_gather x1, waiting for transfers between devices, shards(): weights = lax.all_gather(conv_kernel, 'lon', axis=2, tiled=True)  155 us
    all_gather x1, waiting for transfers between devices, shards(): up_full = lax.all_gather(up_kernel, 'lon', axis=3, tiled=True)  147 us
    reduce_scatter x1, waiting for transfers between devices, shards(): lax.psum_scatter(local_fine.astype(jnp.bfloat16), 'ch', scatter_dimension...  47.2 us
    dot_general x25, matrix products, tap_dot(): jnp.einsum('rbjc,cn->rbjn', piece, weight, preferred_element_type=jnp.flo...  21.6 us
    unnamed x42, local copies, waits for them, and re-layouts  18.6 us
    ppermute x3, starting transfers between devices, padded_2(): lax.ppermute(lax.slice_in_dim(block, 0, width, axis=dim), axis, backward)  11.6 us
  transfers between devices with their start and end apart: 9, of which 7 were waited for; matrix products, arithmetic and copies ran while one was open for 1% of the time, Pallas kernels for 0%

commit v1 on v0

--- a/solution.py
+++ b/solution.py
@@ -64,7 +64,9 @@
     hidden = jax.nn.gelu(summed + up_bias, approximate=False).astype(jnp.bfloat16)
     widened = padded_2(hidden, (("lon", 2),), 1, True)
     framed = padded_2(widened, (("ch", 0),), 1, False)
-    weights = lax.all_gather(conv_kernel, "lon", axis=2, tiled=True)
+    weights = jnp.concatenate(
+        lax.all_to_all(jnp.stack([conv_kernel] * lax.axis_size("lon")), "lon", 0, 0), axis=2
+    )
     band_rows = hidden.shape[0]
     fine_cols = hidden.shape[2]
     result = jnp.zeros(hidden.shape, jnp.float32) + conv_bias

time: 453 us -> 374 us (0.83)
  the two profiles are of different devices: /device:TPU:2 before, /device:TPU:63 now
where the time goes in v1:
time: 374 us; the launch traced here: 373 us
  waiting for transfers between devices  273 us (73%)
  starting transfers between devices  39.6 us (11%)
  local copies, waits for them, and re-layouts  33.4 us (9%)
  between operations  13.9 us (4%)
  matrix products  6.78 us (2%)
  other arithmetic  6.54 us (2%)
    all_gather x1, waiting for transfers between devices, shards(): up_full = lax.all_gather(up_kernel, 'lon', axis=3, tiled=True)  206 us
    reduce_scatter x1, waiting for transfers between devices, shards(): lax.psum_scatter(local_fine.astype(jnp.bfloat16), 'ch', scatter_dimension...  43.3 us
    ppermute x3, waiting for transfers between devices, padded_2(): lax.ppermute(lax.slice_in_dim(block, 0, width, axis=dim), axis, backward)  23.7 us
    all_to_all x1, starting transfers between devices, shards(): lax.all_to_all(jnp.stack([conv_kernel] * lax.axis_size('lon')), 'lon', 0, 0)  18.1 us
    ppermute x3, starting transfers between devices, padded_2(): lax.ppermute(lax.slice_in_dim(block, block.shape[dim] - width, None, axis...  11.9 us
    ppermute x3, starting transfers between devices, padded_2(): lax.ppermute(lax.slice_in_dim(block, 0, width, axis=dim), axis, backward)  9.54 us
    unnamed x32, local copies, waits for them, and re-layouts  8.98 us
    slice x1, local copies, waits for them, and re-layouts, upsample(): term = tap_dot(piece, weights[a, c])  8.85 us
  transfers between devices with their start and end apart: 9, of which 5 were waited for; matrix products, arithmetic and copies ran while one was open for 11% of the time, Pallas kernels for 0%

profile of v1, /device:TPU:63, one launch (start us, length us, event | category | flops | bytes accessed | tf_op | source)
XLA Modules:
  0.0 373.1 jit_solution(9731613115937419185)
XLA Ops:
  6.5 1.4 copy.15
  7.9 3.4 stack.29
  11.3 18.1 %all-to-all-start = ((bf16[64,3,3,8,512]{4,3,2,1,0:T(8,128)(2,1)}), bf16[64,3,3,8,512]{4,3,2,1,0:T(8,128)(2,1)}, u32[]{:S(2)}, u32[]{:S(2)}) async-start(bf16[64,3,3,8,512]{4,3,2,1,0:T(8,128)(2,1)} %stack.29), calls=%async_computation.1 | async-start | bytes 9437184 | tf_op jit(solution)/shard_map/all_to_all | solution.py:68
  29.5 205.8 %all-gather.2.cloned.1.call-done = bf16[4,4,128,512]{2,1,0,3:T(4,128)(2,1)} async-done(((bf16[4,4,128,8]{2,1,0,3:T(4,128)(2,1)}), bf16[4,4,128,512]{2,1,0,3:T(4,128)(2,1)}) %all-gather.2.cloned.1.call-update) | async-done | bytes 2097168 | tf_op jit(solution)/shard_map/all_gather | solution.py:52
  235.3 8.9 %fusion.77 = (bf16[1,1,128,512]{2,1,0,3:T(2,128)(2,1)}, bf16[1,1,128,512]{2,1,0,3:T(2,128)(2,1)}, bf16[1,1,128,512]{2,1,0,3:T(2,128)(2,1)}, bf16[1,1,128,512]{2,...) fusion(bf16[4,4,128,512]{2,1,0,3:T(4,128)(2,1)} %all-gather.2.c, ...), kind=kLoop, calls=%fused_computation.134 | loop fusion | bytes 4194304 | tf_op jit(solution)/shard_map/slice | solution.py:39
  244.2 1.7 copy.65
  245.9 1.7 copy.76
  247.7 1.7 copy.75
  249.4 0.8 copy.74
  250.3 0.1 copy.72
  250.5 0.1 copy.71
  250.6 0.1 copy.70
  250.7 0.1 copy.69
  250.9 0.1 copy.68
  251.8 0.2 fusion.60
  252.1 0.2 convolution_add_fusion.11
  252.3 0.2 convolution_add_fusion.10
  252.6 0.2 fusion.3
  252.8 0.2 fusion.55
  253.1 0.2 convolution_add_fusion.8
  253.3 0.2 convolution_add_fusion.7
  253.6 0.2 fusion.2
  253.9 0.2 fusion.50
  254.1 0.2 convolution_add_fusion.5
  254.4 0.2 convolution_add_fusion.4
  254.6 0.2 fusion.1
  254.9 0.2 fusion.45
  255.1 0.2 convolution_add_fusion.2
  255.4 0.2 convolution_add_fusion.1
  255.6 0.2 fusion
  255.9 0.6 maximum_bitcast_fusion
  256.5 0.3 pad_maximum_fusion
  256.8 2.0 copy.32
  258.8 0.9 copy.80
  259.7 0.5 fusion.76
  260.2 1.9 collective-permute-start
  262.2 3.5 collective-permute-start.1
  265.7 1.3 copy.33
  267.0 0.5 slice.296
  267.5 11.3 %collective-permute-done.1 = bf16[32,4,1,512]{3,2,1,0:T(2,128)(2,1)S(1)} collective-permute-done((bf16[32,4,1,512]{3,2,1,0:T(2,128)(2,1)S(1)}, bf16[32,4,1,512]{3,2,1,0:T(2,128)(2,1)S(1)}, u32[]{:S(2)}, u32[]{:S(2)}) %collective-permute-start.1) | collective-permute-done | bytes 131104 | tf_op jit(solution)/shard_map/ppermute | solution.py:19
  278.8 1.4 convert_add_fusion
  280.2 2.1 scatter-add.6
  282.3 1.4 fusion.23
  283.7 2.1 scatter-add.9
  285.8 1.2 convert_element_type.21
  287.0 43.3 %reduce-scatter.2.cloned.1.call-done = bf16[4,4,8,512]{3,2,1,0:T(8,128)(2,1)} async-done(((bf16[32,4,8,512]{3,2,1,0:T(8,128)(2,1)}), bf16[4,4,8,512]{3,2,1,0:T(8,128)(2,1)}) %reduce-scatter.2.cloned.1.call-update) | async-done | bytes 131088 | tf_op jit(solution)/shard_map/reduce_scatter | solution.py:61
  330.3 1.5 fusion.21
  331.8 7.4 %collective-permute-start.2 = (bf16[4,4,1,512]{3,2,1,0:T(2,128)(2,1)S(1)}, bf16[4,4,1,512]{3,2,1,0:T(2,128)(2,1)S(1)}, u32[]{:S(2)}, u32[]{:S(2)}) collective-permute-start(bf16[4,4,1,512]{3,2,1,0:T(2,128)(2,1)S(1)} %get-tuple-element.51), channel_id=1, source_target_pairs={{0,8},{8,16},{16,24},{24,32},{32,40},{40,48},{48,56},{56,64},{64,7... | collective-permute-start | bytes 49160 | tf_op jit(solution)/shard_map/ppermute | solution.py:16
  339.3 1.9 collective-permute-start.3
  341.2 10.9 %collective-permute-done.3 = bf16[4,4,1,512]{3,2,1,0:T(2,128)(2,1)S(1)} collective-permute-done((bf16[4,4,1,512]{3,2,1,0:T(2,128)(2,1)S(1)}, bf16[4,4,1,512]{3,2,1,0:T(2,128)(2,1)S(1)}, u32[]{:S(2)}, u32[]{:S(2)}) %collective-permute-start.3) | collective-permute-done | bytes 16416 | tf_op jit(solution)/shard_map/ppermute | solution.py:19
  352.2 2.5 collective-permute-start.4
  354.8 4.1 %collective-permute-start.5 = (bf16[1,4,10,512]{3,2,1,0:T(8,128)(2,1)S(1)}, bf16[1,4,10,512]{3,2,1,0:T(8,128)(2,1)S(1)}, u32[]{:S(2)}, u32[]{:S(2)}) collective-permute-start(bf16[1,4,10,512]{3,2,1,0:T(8,128)(2,1)S(1)} %get-tuple-element.50), channel_id=1, source_target_pairs={{1,0},{2,1},{3,2},{4,3},{5,4},{6,5},{7,6},{9,8},{10,9},{11,10},{12... | collective-permute-start | bytes 122888 | tf_op jit(solution)/shard_map/ppermute | solution.py:19
  358.8 1.5 collective-permute-done.5
  360.3 0.2 maximum_maximum_fusion
  360.6 2.7 copy_bitcast_fusion
  363.4 0.2 fusion.12
  363.6 0.2 fusion.13
  363.8 0.2 fusion.14
  364.1 0.2 fusion.15
  364.3 0.2 fusion.17
  364.6 0.2 fusion.18
  364.8 0.2 fusion.16
  365.1 0.3 fusion.10
  365.4 0.9 fusion.11
  (32 shorter events, 1.2 us)
Async XLA Ops:
  6.5 228.8 %all-gather.2.cloned.1.call-start = ((), (), s32[]{:S(2)}) async-start(), calls=%async_computation.2 | async-start | bytes 2129920 | tf_op jit(solution)/shard_map/all_gather | solution.py:52
  11.3 18.1 %copy-start.4 = (bf16[16,4,4,128]{3,2,1,0:T(4,128)(2,1)S(1)}, bf16[16,4,4,128]{3,2,1,0:T(4,128)(2,1)}, u32[]{:S(2)}) copy-start(bf16[16,4,4,128]{3,2,1,0:T(4,128)(2,1)} %param.9) | copy-start | bytes 196612
  11.3 349.3 %all-to-all-start = ((bf16[64,3,3,8,512]{4,3,2,1,0:T(8,128)(2,1)}), bf16[64,3,3,8,512]{4,3,2,1,0:T(8,128)(2,1)}, u32[]{:S(2)}, u32[]{:S(2)}) async-start(bf16[64,3,3,8,512]{4,3,2,1,0:T(8,128)(2,1)} %stack.29), calls=%async_computation.1 | async-start | bytes 9437184 | tf_op jit(solution)/shard_map/all_to_all | solution.py:68
  29.4 300.9 %reduce-scatter.2.cloned.1.call-start = ((), (), s32[]{:S(2)}) async-start(), calls=%async_computation.3 | async-start | bytes 1179648 | tf_op jit(solution)/shard_map/reduce_scatter | solution.py:61
  250.2 2.4 copy-start.3
  253.3 1.5 copy-start.2
  253.6 1.5 copy-start.1
  253.9 1.5 copy-start
  260.2 7.3 %collective-permute-start = (bf16[32,4,1,512]{3,2,1,0:T(2,128)(2,1)S(1)}, bf16[32,4,1,512]{3,2,1,0:T(2,128)(2,1)S(1)}, u32[]{:S(2)}, u32[]{:S(2)}) collective-permute-start(bf16[32,4,1,512]{3,2,1,0:T(2,128)(2,1)S(1)} %get-tuple-element.29), channel_id=1, source_target_pairs={{0,8},{8,16},{16,24},{24,32},{32,40},{40,48},{48,56},{56,64},{64,7... | collective-permute-start | bytes 393224 | tf_op jit(solution)/shard_map/ppermute | solution.py:16
  262.2 16.6 %collective-permute-start.1 = (bf16[32,4,1,512]{3,2,1,0:T(2,128)(2,1)S(1)}, bf16[32,4,1,512]{3,2,1,0:T(2,128)(2,1)S(1)}, u32[]{:S(2)}, u32[]{:S(2)}) collective-permute-start(bf16[32,4,1,512]{3,2,1,0:T(2,128)(2,1)S(1)} %get-tuple-element.30), channel_id=1, source_target_pairs={{8,0},{16,8},{24,16},{32,24},{40,32},{48,40},{56,48},{64,56},{72,6... | collective-permute-start | bytes 393224 | tf_op jit(solution)/shard_map/ppermute | solution.py:19
  267.5 62.8 %copy-start.5 = (f32[512]{0:T(512)S(1)}, f32[512]{0:T(512)}, u32[]{:S(2)}) copy-start(f32[512]{0:T(512)} %param.11) | copy-start | bytes 6148
  331.8 9.4 %collective-permute-start.2 = (bf16[4,4,1,512]{3,2,1,0:T(2,128)(2,1)S(1)}, bf16[4,4,1,512]{3,2,1,0:T(2,128)(2,1)S(1)}, u32[]{:S(2)}, u32[]{:S(2)}) collective-permute-start(bf16[4,4,1,512]{3,2,1,0:T(2,128)(2,1)S(1)} %get-tuple-element.51), channel_id=1, source_target_pairs={{0,8},{8,16},{16,24},{24,32},{32,40},{40,48},{48,56},{56,64},{64,7... | collective-permute-start | bytes 49160 | tf_op jit(solution)/shard_map/ppermute | solution.py:16
  339.3 12.9 %collective-permute-start.3 = (bf16[4,4,1,512]{3,2,1,0:T(2,128)(2,1)S(1)}, bf16[4,4,1,512]{3,2,1,0:T(2,128)(2,1)S(1)}, u32[]{:S(2)}, u32[]{:S(2)}) collective-permute-start(bf16[4,4,1,512]{3,2,1,0:T(2,128)(2,1)S(1)} %get-tuple-element.52), channel_id=1, source_target_pairs={{8,0},{16,8},{24,16},{32,24},{40,32},{48,40},{56,48},{64,56},{72,6... | collective-permute-start | bytes 49160 | tf_op jit(solution)/shard_map/ppermute | solution.py:19
  352.2 6.6 %collective-permute-start.4 = (bf16[1,4,10,512]{3,2,1,0:T(8,128)(2,1)S(1)}, bf16[1,4,10,512]{3,2,1,0:T(8,128)(2,1)S(1)}, u32[]{:S(2)}, u32[]{:S(2)}) collective-permute-start(bf16[1,4,10,512]{3,2,1,0:T(8,128)(2,1)S(1)} %get-tuple-element.49), channel_id=1, source_target_pairs={{0,1},{1,2},{2,3},{3,4},{4,5},{5,6},{6,7},{8,9},{9,10},{10,11},{11... | collective-permute-start | bytes 122888 | tf_op jit(solution)/shard_map/ppermute | solution.py:16
  354.8 5.6 %collective-permute-start.5 = (bf16[1,4,10,512]{3,2,1,0:T(8,128)(2,1)S(1)}, bf16[1,4,10,512]{3,2,1,0:T(8,128)(2,1)S(1)}, u32[]{:S(2)}, u32[]{:S(2)}) collective-permute-start(bf16[1,4,10,512]{3,2,1,0:T(8,128)(2,1)S(1)} %get-tuple-element.50), channel_id=1, source_target_pairs={{1,0},{2,1},{3,2},{4,3},{5,4},{6,5},{7,6},{9,8},{10,9},{11,10},{12... | collective-permute-start | bytes 122888 | tf_op jit(solution)/shard_map/ppermute | solution.py:19
  363.3 1.7 copy-start.6
Sparse Core Ops, SparseCore 0:
  11.8 223.4 all-gather.1
  287.1 43.1 reduce-scatter.1
